TPU v7x, 32 devices: a whole 2x2x4 slice. The times are simulated.
32 devices in a mesh: groups: 2 (over x), row: 16 (over z, y, core).
Axes of the slice: x: 2, y: 2, z: 4, core: 2. Of those that a mesh axis runs over, the one named last changes fastest.
Arguments:
- tensor: float32 [256, 128, 128], P(('groups', 'row')), parts along dimension 0, may hold values from -6 to 6
- init_second: float32 [256, 512], P('groups'), parts along dimension 0, may hold values from -6 to 6
- init_third: float32 [256, 512], P('groups'), parts along dimension 0, may hold values from -6 to 6
Outputs:
- factor_first: float32 [256, 512], P(('groups', 'row')), parts along dimension 0
- factor_second: float32 [256, 512], P(('groups', 'row')), parts along dimension 0
- factor_third: float32 [256, 512], P('groups'), parts along dimension 0
- weights: float32 [1024], P('groups'), parts along dimension 0
There are 2 independent parts, one for each index of `groups`. A program takes and returns all parts, laid end to end along the dimension named above; each array names one. Nothing has to cross between parts.
All inputs are finite; a program needn't handle non-finite values.
Results may differ from a plain program's by a relative error of at most 0.0001.
Values sent between devices are 32-bit elements; how exact they have to be, the bound alone decides.
A program may use at most 128 MiB of HBM per device.

v0:
```python
import math
import jax
import jax.numpy as jnp
from jax import lax
from jax.sharding import PartitionSpec as P

HIGHEST = lax.Precision.HIGHEST
RIDGE = 0.05
EPSILON = 1e-06


def plain_gram(factor):
    return jnp.dot(factor.T, factor, precision=HIGHEST, preferred_element_type=jnp.float32)


def ridge_solve(right, first, second):
    hadamard = first * second
    shift = RIDGE * jnp.mean(jnp.diagonal(hadamard))
    system = hadamard + shift * jnp.eye(hadamard.shape[0], dtype=jnp.float32)
    lower = jnp.linalg.cholesky(system)
    return jax.scipy.linalg.cho_solve((lower, True), right.T).T


def column_scales(gram_raw):
    return jnp.sqrt(jnp.diagonal(gram_raw) + EPSILON)


def on_device(tensor, init_second, init_third):
    local_rows, second_cells, depth_cells = tensor.shape
    factor_cols = init_second.shape[1]
    devices = lax.axis_size("row")
    total_first = local_rows * devices
    gram_b0 = plain_gram(init_second) / second_cells
    gram_c0 = plain_gram(init_third) / depth_cells
    contracted = jnp.einsum("ijk,kr->ijr", tensor, init_third, precision=HIGHEST)
    right_a = jnp.einsum("ijr,jr->ir", contracted, init_second, precision=HIGHEST)
    raw_a = ridge_solve(right_a, gram_b0, gram_c0)
    gram_raw_a = lax.psum(plain_gram(raw_a), "row") / total_first
    scales_a = column_scales(gram_raw_a)
    factor_first = raw_a / scales_a
    gram_a = gram_raw_a / (scales_a[:, None] * scales_a[None, :])
    empty_product = jnp.zeros((local_rows, depth_cells, factor_cols), jnp.float32)
    segment = contracted
    right_own = lax.psum_scatter(
        jnp.einsum("ijr,ir->jr", segment, factor_first, precision=HIGHEST),
        "row",
        scatter_dimension=0,
        tiled=True,
    )
    raw_own = ridge_solve(right_own, gram_a, gram_c0)
    empty_gram = jnp.zeros((factor_cols, factor_cols), jnp.float32)
    segment = lax.all_gather(raw_own, "row", axis=0, tiled=True)
    product_raw = (empty_product, empty_gram)[0] + jnp.einsum(
        "ijk,jr->ikr", tensor, segment, precision=HIGHEST
    )
    gram_total = plain_gram(segment)
    gram_raw_b = gram_total / second_cells
    scales_b = column_scales(gram_raw_b)
    factor_second = raw_own / scales_b
    product = product_raw / scales_b
    gram_b = gram_raw_b / (scales_b[:, None] * scales_b[None, :])
    right_part = jnp.einsum("ikr,ir->kr", product, factor_first, precision=HIGHEST)
    right_c_own = lax.psum_scatter(right_part, "row", scatter_dimension=0, tiled=True)
    raw_c = lax.all_gather(ridge_solve(right_c_own, gram_a, gram_b), "row", axis=0, tiled=True)
    scales_c = jnp.sqrt(jnp.mean(raw_c * raw_c, axis=0) + EPSILON)
    factor_third = raw_c / scales_c
    weights = scales_c / math.sqrt(total_first * second_cells)
    return (factor_first, factor_second, factor_third, weights)


def solution(mesh):
    in_specs = (P(("groups", "row"), None, None), P("groups", None), P("groups", None))
    out_specs = (
        P(("groups", "row"), None),
        P(("groups", "row"), None),
        P("groups", None),
        P("groups"),
    )
    return jax.shard_map(
        on_device, mesh=mesh, in_specs=in_specs, out_specs=out_specs, check_vma=False
    )
```

profile of v0, /device:TPU:0, one launch (start us, length us, event | category | flops | bytes accessed | tf_op | source)
XLA Modules:
  0.0 632.8 jit_solution(15217960713749262886)
XLA Ops:
  12.4 4.7 gather_fusion
  22.4 11.7 %cholesky.374 = f32[128,128]{1,0:T(8,128)S(1)} custom-call(f32[128,128]{1,0:T(8,128)S(1)} %cholesky.586), custom_call_target="Cholesky" | custom-call | tf_op jit(solution)/shard_map/jit(cholesky)/cholesky | solution.py:20
  34.1 9.8 %custom-call.43 = f32[1,128,128]{1,2,0:T(8,128)S(1)} custom-call(f32[1,128,128]{2,1,0:T(8,128)S(1)} %get-tuple-element.88), custom_call_target="InvertDiagBlocksLowerTriangular" | custom-call | tf_op jit(solution)/shard_map/jit(cholesky)/cholesky | solution.py:20
  46.6 11.7 %cholesky.393 = f32[128,128]{1,0:T(8,128)S(1)} custom-call(f32[128,128]{1,0:T(8,128)S(1)} %cholesky.590), custom_call_target="Cholesky" | custom-call | tf_op jit(solution)/shard_map/jit(cholesky)/cholesky | solution.py:20
  58.3 10.0 %custom-call.44 = f32[1,128,128]{1,2,0:T(8,128)S(1)} custom-call(f32[1,128,128]{2,1,0:T(8,128)S(1)} %get-tuple-element.85), custom_call_target="InvertDiagBlocksLowerTriangular" | custom-call | tf_op jit(solution)/shard_map/jit(cholesky)/cholesky | solution.py:20
  69.9 11.7 %cholesky.414 = f32[128,128]{1,0:T(8,128)S(1)} custom-call(f32[128,128]{1,0:T(8,128)S(1)} %cholesky.595), custom_call_target="Cholesky" | custom-call | tf_op jit(solution)/shard_map/jit(cholesky)/cholesky | solution.py:20
  82.4 9.8 %custom-call.45 = f32[1,128,128]{1,2,0:T(8,128)S(1)} custom-call(f32[1,128,128]{2,1,0:T(8,128)S(1)} %get-tuple-element.82), custom_call_target="InvertDiagBlocksLowerTriangular" | custom-call | tf_op jit(solution)/shard_map/jit(cholesky)/cholesky | solution.py:20
  93.6 11.7 %cholesky.431 = f32[128,128]{1,0:T(8,128)S(1)} custom-call(f32[128,128]{1,0:T(8,128)S(1)} %convolution_subtract_fusion.8), custom_call_target="Cholesky" | custom-call | tf_op jit(solution)/shard_map/jit(cholesky)/cholesky | solution.py:20
  110.0 8.0 %while.6 = (s32[]{:T(128)}, f32[512,512]{1,0:T(8,128)S(1)}, s32[4,2]{0,1:T(2,128)S(1)}, f32[4,128,128]{2,1,0:T(8,128)S(1)}, s32[]{:T(128)}) while((s32[]{:T(128)}, f32[512,512]{1,0:T(8,128)S(1)}, s32[4,2]{0,1:T(2,128)S(1)}, f32[4,128,128]{2,1,0:T(8,128)S(1)}, s32[]{:T(128)}) %tuple.78), condition=%wide.while_cond, body=%wide.while_body.sunk | while | flops 2 | bytes 131189 | solution.py:21
  118.0 39.3 %custom-call.46 = f32[4,128,128]{1,2,0:T(8,128)S(1)} custom-call(f32[4,128,128]{2,1,0:T(8,128)S(1)} %get-tuple-element.26), custom_call_target="InvertDiagBlocksLowerTriangular" | custom-call | tf_op jit(solution)/shard_map/jit(_cho_solve)/triangular_solve | solution.py:21
  165.7 96.7 %all-reduce.3.cloned.1.call-done = f32[512,512]{0,1:T(8,128)} async-done(((f32[512,512]{0,1:T(8,128)}), f32[512,512]{0,1:T(8,128)}) %all-reduce.3.cloned.1.call-update) | async-done | bytes 1048592 | tf_op jit(solution)/shard_map/psum | solution.py:38
  281.3 11.7 %cholesky.446 = f32[128,128]{1,0:T(8,128)S(1)} custom-call(f32[128,128]{1,0:T(8,128)S(1)} %cholesky.599), custom_call_target="Cholesky" | custom-call | tf_op jit(solution)/shard_map/jit(cholesky)/cholesky | solution.py:20
  293.7 9.8 %custom-call.47 = f32[1,128,128]{1,2,0:T(8,128)S(1)} custom-call(f32[1,128,128]{2,1,0:T(8,128)S(1)} %get-tuple-element.78), custom_call_target="InvertDiagBlocksLowerTriangular" | custom-call | tf_op jit(solution)/shard_map/jit(cholesky)/cholesky | solution.py:20
  304.3 11.7 %cholesky.465 = f32[128,128]{1,0:T(8,128)S(1)} custom-call(f32[128,128]{1,0:T(8,128)S(1)} %cholesky.603), custom_call_target="Cholesky" | custom-call | tf_op jit(solution)/shard_map/jit(cholesky)/cholesky | solution.py:20
  316.7 10.0 %custom-call.48 = f32[1,128,128]{1,2,0:T(8,128)S(1)} custom-call(f32[1,128,128]{2,1,0:T(8,128)S(1)} %get-tuple-element.75), custom_call_target="InvertDiagBlocksLowerTriangular" | custom-call | tf_op jit(solution)/shard_map/jit(cholesky)/cholesky | solution.py:20
  327.3 11.7 %cholesky.486 = f32[128,128]{1,0:T(8,128)S(1)} custom-call(f32[128,128]{1,0:T(8,128)S(1)} %cholesky.608), custom_call_target="Cholesky" | custom-call | tf_op jit(solution)/shard_map/jit(cholesky)/cholesky | solution.py:20
  339.8 9.8 %custom-call.49 = f32[1,128,128]{1,2,0:T(8,128)S(1)} custom-call(f32[1,128,128]{2,1,0:T(8,128)S(1)} %get-tuple-element.72), custom_call_target="InvertDiagBlocksLowerTriangular" | custom-call | tf_op jit(solution)/shard_map/jit(cholesky)/cholesky | solution.py:20
  350.2 11.7 %cholesky.503 = f32[128,128]{1,0:T(8,128)S(1)} custom-call(f32[128,128]{1,0:T(8,128)S(1)} %convolution_subtract_fusion.7), custom_call_target="Cholesky" | custom-call | tf_op jit(solution)/shard_map/jit(cholesky)/cholesky | solution.py:20
  365.5 7.7 %while.7 = (s32[]{:T(128)}, f32[512,512]{1,0:T(8,128)S(1)}, s32[4,2]{0,1:T(2,128)S(1)}, f32[4,128,128]{2,1,0:T(8,128)S(1)}, s32[]{:T(128)}) while((s32[]{:T(128)}, f32[512,512]{1,0:T(8,128)S(1)}, s32[4,2]{0,1:T(2,128)S(1)}, f32[4,128,128]{2,1,0:T(8,128)S(1)}, s32[]{:T(128)}) %tuple.93), condition=%wide.while_cond.clone, body=%wide.while_body.clone.sunk | while | flops 2 | bytes 131189 | solution.py:21
  373.4 39.3 %custom-call.50 = f32[4,128,128]{1,2,0:T(8,128)S(1)} custom-call(f32[4,128,128]{2,1,0:T(8,128)S(1)} %get-tuple-element.27), custom_call_target="InvertDiagBlocksLowerTriangular" | custom-call | tf_op jit(solution)/shard_map/jit(_cho_solve)/triangular_solve | solution.py:21
  418.3 20.2 %all_gather.6 = f32[128,512]{1,0:T(8,128)S(1)} all-gather(f32[8,512]{1,0:T(8,128)S(1)} %maximum_bitcast_fusion), channel_id=1, replica_groups=mesh['groups'=2,'row'=16] {'row'}, dimensions={0}, use_global_device_ids=true | all-gather | bytes 278528 | tf_op jit(solution)/shard_map/all_gather | solution.py:52
  456.6 11.7 %cholesky.518 = f32[128,128]{1,0:T(8,128)S(1)} custom-call(f32[128,128]{1,0:T(8,128)S(1)} %cholesky.612), custom_call_target="Cholesky" | custom-call | tf_op jit(solution)/shard_map/jit(cholesky)/cholesky | solution.py:20
  469.0 9.8 %custom-call.51 = f32[1,128,128]{1,2,0:T(8,128)S(1)} custom-call(f32[1,128,128]{2,1,0:T(8,128)S(1)} %get-tuple-element.68), custom_call_target="InvertDiagBlocksLowerTriangular" | custom-call | tf_op jit(solution)/shard_map/jit(cholesky)/cholesky | solution.py:20
  479.6 11.7 %cholesky.537 = f32[128,128]{1,0:T(8,128)S(1)} custom-call(f32[128,128]{1,0:T(8,128)S(1)} %cholesky.616), custom_call_target="Cholesky" | custom-call | tf_op jit(solution)/shard_map/jit(cholesky)/cholesky | solution.py:20
  492.0 10.0 %custom-call.52 = f32[1,128,128]{1,2,0:T(8,128)S(1)} custom-call(f32[1,128,128]{2,1,0:T(8,128)S(1)} %get-tuple-element.65), custom_call_target="InvertDiagBlocksLowerTriangular" | custom-call | tf_op jit(solution)/shard_map/jit(cholesky)/cholesky | solution.py:20
  502.7 11.7 %cholesky.558 = f32[128,128]{1,0:T(8,128)S(1)} custom-call(f32[128,128]{1,0:T(8,128)S(1)} %cholesky.621), custom_call_target="Cholesky" | custom-call | tf_op jit(solution)/shard_map/jit(cholesky)/cholesky | solution.py:20
  515.1 9.8 %custom-call.53 = f32[1,128,128]{1,2,0:T(8,128)S(1)} custom-call(f32[1,128,128]{2,1,0:T(8,128)S(1)} %get-tuple-element.62), custom_call_target="InvertDiagBlocksLowerTriangular" | custom-call | tf_op jit(solution)/shard_map/jit(cholesky)/cholesky | solution.py:20
  525.5 11.7 %cholesky.575 = f32[128,128]{1,0:T(8,128)S(1)} custom-call(f32[128,128]{1,0:T(8,128)S(1)} %convolution_subtract_fusion.6), custom_call_target="Cholesky" | custom-call | tf_op jit(solution)/shard_map/jit(cholesky)/cholesky | solution.py:20
  537.9 6.5 %fusion = f32[512,1,128]{2,1,0:T(1,128)S(1)} fusion(f32[8,512,1]{0,2,1:T(1,128)S(1)} %copy.47, f32[8,128,512]{1,2,0:T(8,128)} %divide_bitcast_fusion), kind=kOutput, calls=%fused_computation.11 | convolution fusion | flops 6291456 | bytes 2375680 | tf_op jit(solution)/shard_map/ikr,ir->kr/dot_general | solution.py:62
  547.9 7.7 %while.8 = (s32[]{:T(128)}, f32[512,512]{1,0:T(8,128)S(1)}, s32[4,2]{0,1:T(2,128)S(1)}, f32[4,128,128]{2,1,0:T(8,128)S(1)}, s32[]{:T(128)}) while((s32[]{:T(128)}, f32[512,512]{1,0:T(8,128)S(1)}, s32[4,2]{0,1:T(2,128)S(1)}, f32[4,128,128]{2,1,0:T(8,128)S(1)}, s32[]{:T(128)}) %tuple.94), condition=%wide.while_cond.clone.1, body=%wide.while_body.clone.1.sunk | while | flops 2 | bytes 131189 | solution.py:21
  555.6 39.3 %custom-call.54 = f32[4,128,128]{1,2,0:T(8,128)S(1)} custom-call(f32[4,128,128]{2,1,0:T(8,128)S(1)} %get-tuple-element.28), custom_call_target="InvertDiagBlocksLowerTriangular" | custom-call | tf_op jit(solution)/shard_map/jit(_cho_solve)/triangular_solve | solution.py:21
  604.4 20.2 %all_gather.7 = f32[128,512]{1,0:T(8,128)S(1)} all-gather(f32[8,512]{1,0:T(8,128)S(1)} %maximum_bitcast_fusion.1), channel_id=1, replica_groups=mesh['groups'=2,'row'=16] {'row'}, dimensions={0}, use_global_device_ids=true | all-gather | bytes 278528 | tf_op jit(solution)/shard_map/all_gather | solution.py:64
  (201 shorter events, 112.8 us)
Async XLA Ops:
  7.2 150.2 %copy-start = (f32[8,128,128]{2,1,0:T(8,128)S(1)}, f32[8,128,128]{2,1,0:T(8,128)}, u32[]{:S(2)}) copy-start(f32[8,128,128]{2,1,0:T(8,128)} %param.6) | copy-start | bytes 1572868
  7.2 255.1 %all-reduce.3.cloned.1.call-start = ((), (), s32[]{:S(2)}) async-start(), calls=%async_computation.2 | async-start | bytes 2097152 | tf_op jit(solution)/shard_map/psum | solution.py:38
  9.4 1.0 copy-start.3
  21.3 1.0 copy-start.4
  69.9 87.5 %copy-start.5 = (f32[128,512]{1,0:T(8,128)S(1)}, f32[128,512]{1,0:T(8,128)}, u32[]{:S(2)}) copy-start(f32[128,512]{1,0:T(8,128)} %param.8) | copy-start | bytes 786436
  69.9 87.5 %copy-start.6 = (f32[128,512]{1,0:T(8,128)S(1)}, f32[128,512]{1,0:T(8,128)}, u32[]{:S(2)}) copy-start(f32[128,512]{1,0:T(8,128)} %param.7) | copy-start | bytes 786436
  165.6 247.1 %reduce-scatter.7.cloned.1.call-start = ((), (), s32[]{:S(2)}) async-start(), calls=%async_computation.3 | async-start | bytes 278528 | tf_op jit(solution)/shard_map/reduce_scatter | solution.py:44
  263.6 7.3 %copy-start.1 = (f32[512,512]{0,1:T(8,128)S(1)}, f32[512,512]{0,1:T(8,128)}, u32[]{:S(2)}) copy-start(f32[512,512]{0,1:T(8,128)} %all-reduce.3.cloned.1.call-done) | copy-start | bytes 3145732
  268.2 105.0 %copy-start.7 = (f32[512,8]{0,1:T(8,128)}, f32[512,8]{0,1:T(8,128)S(1)}, u32[]{:S(2)}) copy-start(f32[512,8]{0,1:T(8,128)S(1)} %fusion.115) | copy-start | bytes 49156
  270.9 327.9 %reduce-scatter.9.cloned.1.call-start = ((), (), s32[]{:S(2)}) async-start(), calls=%async_computation.4 | async-start | bytes 278528 | tf_op jit(solution)/shard_map/reduce_scatter | solution.py:63
  444.1 3.2 copy-start.2
Sparse Core Ops, SparseCore 0:
  165.7 96.5 all-reduce.2
  271.0 55.1 reduce-scatter.6
  545.4 53.3 reduce-scatter.8
where the time goes:
time: 636 us; the launch traced here: 633 us
  other arithmetic  371 us (58%)
  waiting for transfers between devices  100 us (16%)
  local copies, waits for them, and re-layouts  53.8 us (8%)
  matrix products  43.5 us (7%)
  blocking collectives  40.4 us (6%)
  between operations  24.2 us (4%)
    another operation x44, other arithmetic, ridge_solve(): lower = jnp.linalg.cholesky(system)  237 us
    another operation x7, other arithmetic, ridge_solve(): return jax.scipy.linalg.cho_solve((lower, True), right.T).T  119 us
    psum x1, waiting for transfers between devices, on_device(): gram_raw_a = lax.psum(plain_gram(raw_a), 'row') / total_first  96.7 us
    another operation x40, local copies, waits for them, and re-layouts, ridge_solve(): return jax.scipy.linalg.cho_solve((lower, True), right.T).T  23.2 us
    all_gather x1, blocking collectives, on_device(): lax.all_gather(ridge_solve(right_c_own, gram_a, gram_b), 'row', axis=0, t...  20.2 us
    all_gather x1, blocking collectives, on_device(): segment = lax.all_gather(raw_own, 'row', axis=0, tiled=True)  20.2 us
    gather x3, local copies, waits for them, and re-layouts, ridge_solve(): shift = RIDGE * jnp.mean(jnp.diagonal(hadamard))  14.2 us
    another operation x42, matrix products, ridge_solve(): return jax.scipy.linalg.cho_solve((lower, True), right.T).T  14.1 us
  transfers between devices with their start and end apart: 3, of which 2 were waited for; matrix products, arithmetic and copies ran while one was open for 29% of the time, Pallas kernels for 0%

commit v1 on v0

--- a/solution.py
+++ b/solution.py
@@ -35,7 +35,7 @@
     contracted = jnp.einsum("ijk,kr->ijr", tensor, init_third, precision=HIGHEST)
     right_a = jnp.einsum("ijr,jr->ir", contracted, init_second, precision=HIGHEST)
     raw_a = ridge_solve(right_a, gram_b0, gram_c0)
-    gram_raw_a = lax.psum(plain_gram(raw_a), "row") / total_first
+    gram_raw_a = jnp.sum(lax.all_gather(plain_gram(raw_a), "row"), axis=0) / total_first
     scales_a = column_scales(gram_raw_a)
     factor_first = raw_a / scales_a
     gram_a = gram_raw_a / (scales_a[:, None] * scales_a[None, :])

time: 636 us -> 685 us (1.077)
  waiting for transfers between devices: 100 us -> 129 us
  other arithmetic: 371 us -> 380 us
  local copies, waits for them, and re-layouts: 53.8 us -> 61.3 us
    all_gather x0 -> x1, waiting for transfers between devices: none -> 129 us  [on_device(): lax.all_gather(plain_gram(raw_a), 'row')]
    psum x1 -> x0, waiting for transfers between devices: 96.7 us -> none  [on_device(): gram_raw_a = lax.psum(plain_gram(raw_a), 'row') / total_first]
    reduce_sum x0 -> x1, other arithmetic: none -> 7.95 us  [on_device(): jnp.sum(lax.all_gather(plain_gram(raw_a), 'row'), axis=0) / total_first]
  transfers between devices with their start and end apart: 3 -> 3, of which waited for: 2 -> 2; matrix products, arithmetic and copies ran while one was open for 29% -> 28% of each run, Pallas kernels for 0% -> 0%
where the time goes in v1:
time: 685 us; the launch traced here: 681 us
  other arithmetic  380 us (55%)
  waiting for transfers between devices  129 us (19%)
  local copies, waits for them, and re-layouts  61.3 us (9%)
  matrix products  47.2 us (7%)
  blocking collectives  38.3 us (6%)
  between operations  24.5 us (4%)
    another operation x44, other arithmetic, ridge_solve(): lower = jnp.linalg.cholesky(system)  237 us
    all_gather x1, waiting for transfers between devices, on_device(): lax.all_gather(plain_gram(raw_a), 'row')  129 us
    another operation x7, other arithmetic, ridge_solve(): return jax.scipy.linalg.cho_solve((lower, True), right.T).T  120 us
    another operation x40, local copies, waits for them, and re-layouts, ridge_solve(): return jax.scipy.linalg.cho_solve((lower, True), right.T).T  27.5 us
    all_gather x1, blocking collectives, on_device(): segment = lax.all_gather(raw_own, 'row', axis=0, tiled=True)  20.1 us
    all_gather x1, blocking collectives, on_device(): lax.all_gather(ridge_solve(right_c_own, gram_a, gram_b), 'row', axis=0, t...  18.2 us
    another operation x42, matrix products, ridge_solve(): return jax.scipy.linalg.cho_solve((lower, True), right.T).T  17.4 us
    gather x3, local copies, waits for them, and re-layouts, ridge_solve(): shift = RIDGE * jnp.mean(jnp.diagonal(hadamard))  14.7 us
  transfers between devices with their start and end apart: 3, of which 2 were waited for; matrix products, arithmetic and copies ran while one was open for 28% of the time, Pallas kernels for 0%

profile of v1, /device:TPU:0, one launch (start us, length us, event | category | flops | bytes accessed | tf_op | source)
XLA Modules:
  0.0 681.4 jit_solution(14470539792063403051)
XLA Ops:
  12.5 5.1 gather_fusion
  21.7 11.7 %cholesky.374 = f32[128,128]{1,0:T(8,128)S(1)} custom-call(f32[128,128]{1,0:T(8,128)S(1)} %cholesky.586), custom_call_target="Cholesky" | custom-call | tf_op jit(solution)/shard_map/jit(cholesky)/cholesky | solution.py:20
  33.5 9.8 %custom-call.43 = f32[1,128,128]{1,2,0:T(8,128)S(1)} custom-call(f32[1,128,128]{2,1,0:T(8,128)S(1)} %get-tuple-element.88), custom_call_target="InvertDiagBlocksLowerTriangular" | custom-call | tf_op jit(solution)/shard_map/jit(cholesky)/cholesky | solution.py:20
  44.1 11.7 %cholesky.393 = f32[128,128]{1,0:T(8,128)S(1)} custom-call(f32[128,128]{1,0:T(8,128)S(1)} %cholesky.590), custom_call_target="Cholesky" | custom-call | tf_op jit(solution)/shard_map/jit(cholesky)/cholesky | solution.py:20
  55.8 10.0 %custom-call.44 = f32[1,128,128]{1,2,0:T(8,128)S(1)} custom-call(f32[1,128,128]{2,1,0:T(8,128)S(1)} %get-tuple-element.85), custom_call_target="InvertDiagBlocksLowerTriangular" | custom-call | tf_op jit(solution)/shard_map/jit(cholesky)/cholesky | solution.py:20
  66.5 11.7 %cholesky.414 = f32[128,128]{1,0:T(8,128)S(1)} custom-call(f32[128,128]{1,0:T(8,128)S(1)} %cholesky.595), custom_call_target="Cholesky" | custom-call | tf_op jit(solution)/shard_map/jit(cholesky)/cholesky | solution.py:20
  79.0 9.8 %custom-call.45 = f32[1,128,128]{1,2,0:T(8,128)S(1)} custom-call(f32[1,128,128]{2,1,0:T(8,128)S(1)} %get-tuple-element.82), custom_call_target="InvertDiagBlocksLowerTriangular" | custom-call | tf_op jit(solution)/shard_map/jit(cholesky)/cholesky | solution.py:20
  89.4 11.7 %cholesky.431 = f32[128,128]{1,0:T(8,128)S(1)} custom-call(f32[128,128]{1,0:T(8,128)S(1)} %convolution_subtract_fusion.8), custom_call_target="Cholesky" | custom-call | tf_op jit(solution)/shard_map/jit(cholesky)/cholesky | solution.py:20
  105.3 8.0 %while.6 = (s32[]{:T(128)}, f32[512,512]{1,0:T(8,128)S(1)}, s32[4,2]{0,1:T(2,128)S(1)}, f32[4,128,128]{2,1,0:T(8,128)S(1)}, s32[]{:T(128)}) while((s32[]{:T(128)}, f32[512,512]{1,0:T(8,128)S(1)}, s32[4,2]{0,1:T(2,128)S(1)}, f32[4,128,128]{2,1,0:T(8,128)S(1)}, s32[]{:T(128)}) %tuple.78), condition=%wide.while_cond, body=%wide.while_body.sunk | while | flops 2 | bytes 131181 | solution.py:21
  113.3 39.3 %custom-call.46 = f32[4,128,128]{1,2,0:T(8,128)S(1)} custom-call(f32[4,128,128]{2,1,0:T(8,128)S(1)} %get-tuple-element.26), custom_call_target="InvertDiagBlocksLowerTriangular" | custom-call | tf_op jit(solution)/shard_map/jit(_cho_solve)/triangular_solve | solution.py:21
  161.0 129.3 %all-gather.3.cloned.1.call-done = f32[8192,512]{1,0:T(8,128)} async-done(((f32[512,512]{1,0:T(8,128)}), f32[8192,512]{1,0:T(8,128)}) %all-gather.3.cloned.1.call-update) | async-done | bytes 16777232 | tf_op jit(solution)/shard_map/all_gather | solution.py:38
  290.3 8.0 %reduce_sum.46 = f32[512,512]{1,0:T(8,128)S(1)} reduce(f32[16,512,512]{2,1,0:T(8,128)} %bitcast.223, f32[]{:T(128)} %constant.145.clone.1), dimensions={0}, to_apply=%region_9.12 | reduce | flops 3932160 | bytes 17825796 | tf_op jit(solution)/shard_map/reduce_sum | solution.py:38
  317.2 11.7 %cholesky.446 = f32[128,128]{1,0:T(8,128)S(1)} custom-call(f32[128,128]{1,0:T(8,128)S(1)} %cholesky.599), custom_call_target="Cholesky" | custom-call | tf_op jit(solution)/shard_map/jit(cholesky)/cholesky | solution.py:20
  329.0 9.8 %custom-call.47 = f32[1,128,128]{1,2,0:T(8,128)S(1)} custom-call(f32[1,128,128]{2,1,0:T(8,128)S(1)} %get-tuple-element.78), custom_call_target="InvertDiagBlocksLowerTriangular" | custom-call | tf_op jit(solution)/shard_map/jit(cholesky)/cholesky | solution.py:20
  341.4 11.7 %cholesky.465 = f32[128,128]{1,0:T(8,128)S(1)} custom-call(f32[128,128]{1,0:T(8,128)S(1)} %cholesky.603), custom_call_target="Cholesky" | custom-call | tf_op jit(solution)/shard_map/jit(cholesky)/cholesky | solution.py:20
  354.4 10.0 %custom-call.48 = f32[1,128,128]{1,2,0:T(8,128)S(1)} custom-call(f32[1,128,128]{2,1,0:T(8,128)S(1)} %get-tuple-element.75), custom_call_target="InvertDiagBlocksLowerTriangular" | custom-call | tf_op jit(solution)/shard_map/jit(cholesky)/cholesky | solution.py:20
  366.0 11.7 %cholesky.486 = f32[128,128]{1,0:T(8,128)S(1)} custom-call(f32[128,128]{1,0:T(8,128)S(1)} %cholesky.608), custom_call_target="Cholesky" | custom-call | tf_op jit(solution)/shard_map/jit(cholesky)/cholesky | solution.py:20
  378.4 9.8 %custom-call.49 = f32[1,128,128]{1,2,0:T(8,128)S(1)} custom-call(f32[1,128,128]{2,1,0:T(8,128)S(1)} %get-tuple-element.72), custom_call_target="InvertDiagBlocksLowerTriangular" | custom-call | tf_op jit(solution)/shard_map/jit(cholesky)/cholesky | solution.py:20
  389.7 11.7 %cholesky.503 = f32[128,128]{1,0:T(8,128)S(1)} custom-call(f32[128,128]{1,0:T(8,128)S(1)} %convolution_subtract_fusion.7), custom_call_target="Cholesky" | custom-call | tf_op jit(solution)/shard_map/jit(cholesky)/cholesky | solution.py:20
  408.8 11.3 %while.7 = (s32[]{:T(128)}, f32[512,512]{1,0:T(8,128)}, s32[4,2]{0,1:T(2,128)S(1)}, f32[4,128,128]{2,1,0:T(8,128)S(1)}, s32[]{:T(128)}) while((s32[]{:T(128)}, f32[512,512]{1,0:T(8,128)}, s32[4,2]{0,1:T(2,128)S(1)}, f32[4,128,128]{2,1,0:T(8,128)S(1)}, s32[]{:T(128)}) %tuple.93), condition=%wide.while_cond.clone, body=%wide.while_body.clone.sunk | while | flops 2 | bytes 131181 | solution.py:21
  420.1 39.3 %custom-call.50 = f32[4,128,128]{1,2,0:T(8,128)S(1)} custom-call(f32[4,128,128]{2,1,0:T(8,128)S(1)} %get-tuple-element.27), custom_call_target="InvertDiagBlocksLowerTriangular" | custom-call | tf_op jit(solution)/shard_map/jit(_cho_solve)/triangular_solve | solution.py:21
  468.6 20.1 %all_gather.14 = f32[128,512]{1,0:T(8,128)S(1)} all-gather(f32[8,512]{1,0:T(8,128)S(1)} %maximum_bitcast_fusion), channel_id=1, replica_groups=mesh['groups'=2,'row'=16] {'row'}, dimensions={0}, use_global_device_ids=true | all-gather | bytes 278528 | tf_op jit(solution)/shard_map/all_gather | solution.py:52
  513.2 11.7 %cholesky.518 = f32[128,128]{1,0:T(8,128)S(1)} custom-call(f32[128,128]{1,0:T(8,128)S(1)} %cholesky.612), custom_call_target="Cholesky" | custom-call | tf_op jit(solution)/shard_map/jit(cholesky)/cholesky | solution.py:20
  525.0 9.8 %custom-call.51 = f32[1,128,128]{1,2,0:T(8,128)S(1)} custom-call(f32[1,128,128]{2,1,0:T(8,128)S(1)} %get-tuple-element.68), custom_call_target="InvertDiagBlocksLowerTriangular" | custom-call | tf_op jit(solution)/shard_map/jit(cholesky)/cholesky | solution.py:20
  537.4 11.7 %cholesky.537 = f32[128,128]{1,0:T(8,128)S(1)} custom-call(f32[128,128]{1,0:T(8,128)S(1)} %cholesky.616), custom_call_target="Cholesky" | custom-call | tf_op jit(solution)/shard_map/jit(cholesky)/cholesky | solution.py:20
  550.4 10.0 %custom-call.52 = f32[1,128,128]{1,2,0:T(8,128)S(1)} custom-call(f32[1,128,128]{2,1,0:T(8,128)S(1)} %get-tuple-element.65), custom_call_target="InvertDiagBlocksLowerTriangular" | custom-call | tf_op jit(solution)/shard_map/jit(cholesky)/cholesky | solution.py:20
  562.0 11.7 %cholesky.558 = f32[128,128]{1,0:T(8,128)S(1)} custom-call(f32[128,128]{1,0:T(8,128)S(1)} %cholesky.621), custom_call_target="Cholesky" | custom-call | tf_op jit(solution)/shard_map/jit(cholesky)/cholesky | solution.py:20
  574.4 9.8 %custom-call.53 = f32[1,128,128]{1,2,0:T(8,128)S(1)} custom-call(f32[1,128,128]{2,1,0:T(8,128)S(1)} %get-tuple-element.62), custom_call_target="InvertDiagBlocksLowerTriangular" | custom-call | tf_op jit(solution)/shard_map/jit(cholesky)/cholesky | solution.py:20
  585.6 11.7 %cholesky.575 = f32[128,128]{1,0:T(8,128)S(1)} custom-call(f32[128,128]{1,0:T(8,128)S(1)} %convolution_subtract_fusion.6), custom_call_target="Cholesky" | custom-call | tf_op jit(solution)/shard_map/jit(cholesky)/cholesky | solution.py:20
  601.0 8.5 %while.8 = (s32[]{:T(128)}, f32[512,512]{1,0:T(8,128)S(1)}, s32[4,2]{0,1:T(2,128)S(1)}, f32[4,128,128]{2,1,0:T(8,128)S(1)}, s32[]{:T(128)}) while((s32[]{:T(128)}, f32[512,512]{1,0:T(8,128)S(1)}, s32[4,2]{0,1:T(2,128)S(1)}, f32[4,128,128]{2,1,0:T(8,128)S(1)}, s32[]{:T(128)}) %tuple.94), condition=%wide.while_cond.clone.1, body=%wide.while_body.clone.1.sunk | while | flops 2 | bytes 131181 | solution.py:21
  609.5 39.3 %custom-call.54 = f32[4,128,128]{1,2,0:T(8,128)S(1)} custom-call(f32[4,128,128]{2,1,0:T(8,128)S(1)} %get-tuple-element.28), custom_call_target="InvertDiagBlocksLowerTriangular" | custom-call | tf_op jit(solution)/shard_map/jit(_cho_solve)/triangular_solve | solution.py:21
  655.1 18.2 %all_gather.15 = f32[128,512]{1,0:T(8,128)S(1)} all-gather(f32[8,512]{1,0:T(8,128)S(1)} %maximum_bitcast_fusion.1), channel_id=1, replica_groups=mesh['groups'=2,'row'=16] {'row'}, dimensions={0}, use_global_device_ids=true | all-gather | bytes 278528 | tf_op jit(solution)/shard_map/all_gather | solution.py:64
  (203 shorter events, 128.9 us)
Async XLA Ops:
  7.2 145.5 %copy-start = (f32[8,128,128]{2,1,0:T(8,128)S(1)}, f32[8,128,128]{2,1,0:T(8,128)}, u32[]{:S(2)}) copy-start(f32[8,128,128]{2,1,0:T(8,128)} %param.6) | copy-start | bytes 1572868
  7.2 283.1 %all-gather.3.cloned.1.call-start = ((), (), s32[]{:S(2)}) async-start(), calls=%async_computation.2 | async-start | bytes 17825792 | tf_op jit(solution)/shard_map/all_gather | solution.py:38
  9.4 1.0 copy-start.2
  66.5 86.2 %copy-start.5 = (f32[128,512]{1,0:T(8,128)S(1)}, f32[128,512]{1,0:T(8,128)}, u32[]{:S(2)}) copy-start(f32[128,512]{1,0:T(8,128)} %param.8) | copy-start | bytes 786436
  66.5 86.2 %copy-start.6 = (f32[128,512]{1,0:T(8,128)S(1)}, f32[128,512]{1,0:T(8,128)}, u32[]{:S(2)}) copy-start(f32[128,512]{1,0:T(8,128)} %param.7) | copy-start | bytes 786436
  161.0 298.7 %reduce-scatter.7.cloned.1.call-start = ((), (), s32[]{:S(2)}) async-start(), calls=%async_computation.3 | async-start | bytes 278528 | tf_op jit(solution)/shard_map/reduce_scatter | solution.py:44
  304.8 154.7 %copy-start.7 = (f32[512,8]{0,1:T(8,128)}, f32[512,8]{0,1:T(8,128)S(1)}, u32[]{:S(2)}) copy-start(f32[512,8]{0,1:T(8,128)S(1)} %fusion.115) | copy-start | bytes 49156
  316.2 1.0 copy-start.3
  405.1 244.3 %reduce-scatter.9.cloned.1.call-start = ((), (), s32[]{:S(2)}) async-start(), calls=%async_computation.4 | async-start | bytes 278528 | tf_op jit(solution)/shard_map/reduce_scatter | solution.py:63
  489.7 4.6 copy-start.1
  512.2 1.0 copy-start.4
Sparse Core Ops, SparseCore 0:
  161.1 129.1 all-gather.2
  405.3 54.3 reduce-scatter.6
  503.4 53.3 reduce-scatter.8
